TPU v7x, 256 devices: a whole 4x4x8 slice. The times are simulated.
256 devices in a mesh: row: 8 (over x_hi, y), col: 32 (over x_lo, z, core).
Axes of the slice: x: 4 (x_hi: 2, x_lo: 2; x = x_hi * 2 + x_lo), y: 4, z: 8, core: 2. Of those that a mesh axis runs over, the one named last changes fastest.
Arguments:
- residuals: bfloat16 [262144, 768], P(('row', 'col')), may hold values from -6 to 6
- codes: int32 [262144, 64], P(('row', 'col')), may hold values from 0 to 255
- list_ids: int32 [262144], P(('row', 'col')), may hold values from 0 to 65535, as said below
- rotation: bfloat16 [768, 768], replicated, may hold values from -0.21875 to 0.21875
- codebook: bfloat16 [256, 768], replicated, may hold values from -6 to 6
- list_fill: int32 [65536], P(('row', 'col')), may hold values from 0 to 4095
Outputs:
- list_drift: float32 [65536, 768], P(('row', 'col'))
- list_counts: int32 [65536], P(('row', 'col'))
- new_blocks: int32 [65536], P(('row', 'col'))
Inputs may be any that keep to these rules, and one draw needn't show every extreme that they name: `list_ids`: lists are grouped in blocks of 256 consecutive ids. Among the rows of one device (aligned blocks of 1024 rows), at most 12 have lists in the same block, and in every such aligned block some list block is named by exactly 12 rows.
All inputs are finite; a program needn't handle non-finite values.
Results may differ from a plain program's by a relative error of at most 0.0029.
Values may be sent and summed in bfloat16 or wider, within the bound.
A program may use at most 64 MiB of HBM per device.

v0:
```python
import jax
import jax.numpy as jnp
from jax import lax
from jax.sharding import PartitionSpec as P


def cut_along(shard, dim, peers):
    shape = shard.shape
    blocks = shard.reshape(*shape[:dim], peers, shape[dim] // peers, *shape[dim + 1 :])
    return jnp.moveaxis(blocks, dim, 0)


def joined_along(blocks, dim):
    shape = list(blocks.shape[1:])
    shape[dim] *= blocks.shape[0]
    return jnp.moveaxis(blocks, 0, dim).reshape(shape)


def one_exchange(shard, axis, axes, splits, concats):
    sizes = [lax.axis_size(a) for a in axes]
    blocks = cut_along(shard, splits[0], sizes[0])
    blocks = jnp.moveaxis(cut_along(blocks, splits[1] + 1, sizes[1]), 0, 1)
    inside = blocks.shape[2:]
    blocks = blocks.reshape(-1, *inside)
    blocks = lax.all_to_all(blocks, axis, split_axis=0, concat_axis=0, tiled=True)
    blocks = joined_along(blocks.reshape(*sizes, *inside), concats[0] + 1)
    return joined_along(blocks, concats[1])


def decode_rows(codes, codebook):
    vec_rows, sub_count = codes.shape
    cent_count, feat_width = codebook.shape
    sub_width = feat_width // sub_count
    code_table = codebook.reshape(cent_count, sub_count, sub_width)
    block_rows = 256
    code_blocks = codes.reshape(vec_rows // block_rows, block_rows, sub_count)

    def one_block(code_block):
        picker = (
            code_block[:, :, None] == jnp.arange(cent_count, dtype=jnp.int32)[None, None, :]
        ).astype(jnp.bfloat16)
        picked = jnp.einsum("bmk,kmj->bmj", picker, code_table, preferred_element_type=jnp.float32)
        return picked.reshape(block_rows, feat_width)

    return lax.map(one_block, code_blocks).reshape(vec_rows, feat_width)


def sum_by_list(rows_in, tags_in, list_total):
    picker = (tags_in[:, None] == jnp.arange(list_total, dtype=jnp.int32)[None, :]).astype(
        jnp.bfloat16
    )
    list_sums = lax.dot_general(
        picker, rows_in, (((0,), (0,)), ((), ())), preferred_element_type=jnp.float32
    )
    counts = jnp.sum(picker, axis=0, dtype=jnp.float32)
    return (list_sums, counts)


def rank_in_block(owner_block, owner_total):
    vec_rows = owner_block.shape[0]
    picker = (owner_block[:, None] == jnp.arange(owner_total, dtype=jnp.int32)[None, :]).astype(
        jnp.bfloat16
    )
    later = (
        jnp.arange(vec_rows, dtype=jnp.int32)[:, None]
        > jnp.arange(vec_rows, dtype=jnp.int32)[None, :]
    )
    before = jnp.dot(later.astype(jnp.bfloat16), picker, preferred_element_type=jnp.float32)
    return jnp.sum(before * picker.astype(jnp.float32), axis=1).astype(jnp.int32)


def local(residuals, codes, list_ids, rotation, codebook, list_fill):
    row_count = lax.axis_size("row")
    col_count = lax.axis_size("col")
    owner_total = row_count * col_count
    vec_rows, feat_width = residuals.shape
    lists_here = list_fill.shape[0]
    slot_cap = 3 * vec_rows // owner_total
    rotated = jnp.dot(residuals, rotation, preferred_element_type=jnp.float32)
    rebuilt = decode_rows(codes, codebook)
    encode_error = (rotated - rebuilt).astype(jnp.bfloat16)
    owner_block = list_ids // lists_here
    slot_index = owner_block * slot_cap + rank_in_block(owner_block, owner_total)
    send_rows = (
        jnp.zeros((owner_total * slot_cap, feat_width), jnp.bfloat16)
        .at[slot_index]
        .set(encode_error)
    )
    send_tags = jnp.full((owner_total * slot_cap,), -1, jnp.int32).at[slot_index].set(list_ids)
    send_rows = send_rows.reshape(row_count, col_count, slot_cap, feat_width)
    send_tags = send_tags.reshape(row_count, col_count, slot_cap)
    got_rows, got_tags = (
        one_exchange(send_rows, ("row", "col"), ("row", "col"), (0, 1), (0, 1)),
        one_exchange(send_tags, ("row", "col"), ("row", "col"), (0, 1), (0, 1)),
    )
    got_rows = got_rows.reshape(-1, feat_width)
    got_tags = got_tags.reshape(-1)
    list_base = (lax.axis_index("row") * col_count + lax.axis_index("col")) * lists_here
    local_index = jnp.where(got_tags >= 0, got_tags - list_base, -1)
    list_sums, counts = sum_by_list(got_rows, local_index, lists_here)
    list_counts = counts.astype(jnp.int32)
    divisor = jnp.maximum(list_counts, 1).astype(jnp.float32)
    list_drift = list_sums / divisor[:, None]
    new_blocks = (list_fill + list_counts + 127) // 128 - (list_fill + 127) // 128
    return (list_drift, list_counts, new_blocks)


def solution(mesh):
    placed = (
        P(("row", "col"), None),
        P(("row", "col"), None),
        P(("row", "col")),
        P(),
        P(),
        P(("row", "col")),
    )
    return jax.shard_map(
        local,
        mesh=mesh,
        in_specs=placed,
        out_specs=(P(("row", "col"), None), P(("row", "col")), P(("row", "col"))),
        check_vma=False,
    )
```

profile of v0, /device:TPU:1, one launch (start us, length us, event | category | flops | bytes accessed | tf_op | source)
XLA Modules:
  0.0 248.3 jit_solution(11712588521732106226)
XLA Ops:
  0.6 0.0 copy-start
  0.6 0.0 copy-start.3
  0.7 0.0 copy-start.2
  0.7 0.0 copy-start.1
  0.7 0.8 add_select_fusion
  1.5 0.8 fusion.11
  2.3 0.0 copy-done.3
  2.3 4.3 %scatter_custom_fusion = s32[3072]{0:T(1024)S(1)} fusion(s32[1024]{0:T(1024)S(1)} %compare_select_fusion.1, s32[1024]{0:T(1024)S(1)} %copy-done.3, s32[]{:T(128)} %constant.57.clone.1), kind=kCustom, calls=%fused_computation.32 | custom fusion | bytes 12292 | tf_op jit(solution)/shard_map/scatter | solution.py:89
  6.7 0.8 reshape_transpose_transpose_reshape_reshape_reshape.6
  7.5 15.6 %all-to-all-start = ((s32[256,1,1,12]{3,2,1,0:T(1,128)}), s32[256,1,1,12]{3,2,1,0:T(1,128)S(1)}, u32[]{:S(2)}, u32[]{:S(2)}) async-start(s32[256,1,1,12]{3,2,1,0:T(1,128)} %bitcast.2), calls=%async_computation | async-start | bytes 262144 | tf_op jit(solution)/shard_map/all_to_all | solution.py:25
  23.2 0.0 copy-done.2
  23.2 0.8 reshape.58
  24.0 0.2 copy.20
  24.2 0.9 reshape.59
  25.0 32.8 %while.10 = (s32[]{:T(128)}, f32[4,256,768]{2,1,0:T(8,128)}, s32[4,256,64]{1,0,2:T(4,128)}, bf16[256,64,12]{0,2,1:T(8,128)(2,1)}, s32[]{:T(128)}) while((s32[]{:T(128)}, f32[4,256,768]{2,1,0:T(8,128)}, s32[4,256,64]{1,0,2:T(4,128)}, bf16[256,64,12]{0,2,1:T(8,128)(2,1)}, s32[]{:T(128)}) %tuple.26), condition=%wide.region_3.4_spmd, body=%wide.region_2.3_spmd.sunk | while | flops 104857600 | bytes 6225997 | solution.py:45
  25.0 1.0 constant_dynamic-slice_fusion.2
  26.1 5.9 %fusion.27 = f32[256,64,12]{0,2,1:T(8,128)S(1)} fusion(bf16[256,64,12]{0,2,1:T(8,128)(2,1)} %get-tuple-element.86, s32[256,64]{0,1:T(8,128)S(1)} %bitcast.48), kind=kOutput, calls=%fused_computation.5.clone.1 | convolution fusion | flops 104857600 | bytes 1245184 | tf_op jit(solution)/shard_map/while/body/eval_jaxpr/bmk,kmj->bmj/dot_general | solution.py:42
  31.9 0.1 broadcast_in_dim.40
  32.0 0.3 copy.34
  32.3 0.9 constant_dynamic-update-slice_fusion.2
  33.2 1.0 constant_dynamic-slice_fusion.2
  34.3 5.9 %fusion.27 = f32[256,64,12]{0,2,1:T(8,128)S(1)} fusion(bf16[256,64,12]{0,2,1:T(8,128)(2,1)} %get-tuple-element.86, s32[256,64]{0,1:T(8,128)S(1)} %bitcast.48), kind=kOutput, calls=%fused_computation.5.clone.1 | convolution fusion | flops 104857600 | bytes 1245184 | tf_op jit(solution)/shard_map/while/body/eval_jaxpr/bmk,kmj->bmj/dot_general | solution.py:42
  40.1 0.1 broadcast_in_dim.40
  40.2 0.3 copy.34
  40.5 1.0 constant_dynamic-update-slice_fusion.2
  41.5 1.0 constant_dynamic-slice_fusion.2
  42.5 5.9 %fusion.27 = f32[256,64,12]{0,2,1:T(8,128)S(1)} fusion(bf16[256,64,12]{0,2,1:T(8,128)(2,1)} %get-tuple-element.86, s32[256,64]{0,1:T(8,128)S(1)} %bitcast.48), kind=kOutput, calls=%fused_computation.5.clone.1 | convolution fusion | flops 104857600 | bytes 1245184 | tf_op jit(solution)/shard_map/while/body/eval_jaxpr/bmk,kmj->bmj/dot_general | solution.py:42
  48.3 0.1 broadcast_in_dim.40
  48.4 0.3 copy.34
  48.7 0.9 constant_dynamic-update-slice_fusion.2
  49.7 1.0 constant_dynamic-slice_fusion.2
  50.7 5.9 %fusion.27 = f32[256,64,12]{0,2,1:T(8,128)S(1)} fusion(bf16[256,64,12]{0,2,1:T(8,128)(2,1)} %get-tuple-element.86, s32[256,64]{0,1:T(8,128)S(1)} %bitcast.48), kind=kOutput, calls=%fused_computation.5.clone.1 | convolution fusion | flops 104857600 | bytes 1245184 | tf_op jit(solution)/shard_map/while/body/eval_jaxpr/bmk,kmj->bmj/dot_general | solution.py:42
  56.6 0.1 broadcast_in_dim.40
  56.6 0.3 copy.34
  56.9 1.0 constant_dynamic-update-slice_fusion.2
  57.9 3.6 %fusion.4 = bf16[1024,768]{1,0:T(8,128)(2,1)S(1)} fusion(f32[4,256,768]{2,1,0:T(8,128)} %get-tuple-element.25, bf16[1024,768]{1,0:T(8,128)(2,1)S(1)} %copy-done, bf16[768,768]{1,0:T(8,128)(2,1)} %param.11), kind=kOutput, calls=%fused_computation.12 | convolution fusion | flops 1209532416 | bytes 7471104 | tf_op jit(solution)/shard_map/dot_general | solution.py:79
  61.5 8.2 %scatter_custom_fusion.1 = bf16[3072,768]{1,0:T(8,128)(2,1)} fusion(s32[1024]{0:T(1024)S(1)} %compare_select_fusion.1, bf16[1024,768]{1,0:T(8,128)(2,1)S(1)} %fusion.4, bf16[]{:T(256)} %constant.70.clone.1), kind=kCustom, calls=%fused_computation.17 | custom fusion | bytes 4718594 | tf_op jit(solution)/shard_map/scatter | solution.py:87
  69.8 8.2 %reshape_transpose_transpose_reshape_reshape_reshape.7 = bf16[256,1,1,12,768]{4,3,0,2,1:T(8,128)(2,1)} reshape(bf16[3072,768]{1,0:T(8,128)(2,1)} %scatter_custom_fusion.1) | data formatting | bytes 9437184 | tf_op jit(solution)/shard_map/reshape;transpose;transpose;reshape;reshape;reshape | solution.py:24
  78.0 0.0 all-to-all-done
  78.0 14.6 %all-to-all-start.1 = ((bf16[256,1,1,12,768]{4,3,2,1,0:T(8,128)(2,1)}), bf16[256,1,1,12,768]{4,3,2,1,0:T(8,128)(2,1)}, u32[]{:S(2)}, u32[]{:S(2)}) async-start(bf16[256,1,1,12,768]{4,3,2,1,0:T(8,128)(2,1)} %bitcast.47), calls=%async_computation.1 | async-start | bytes 12582912 | tf_op jit(solution)/shard_map/all_to_all | solution.py:25
  92.6 0.1 compare_select_fusion
  92.8 0.1 select_n.39
  92.9 1.4 convert_reduce_fusion
  94.3 0.6 fusion.19
  94.9 139.8 %all-to-all-done.1 = bf16[256,1,1,12,768]{4,3,2,1,0:T(8,128)(2,1)} async-done(((bf16[256,1,1,12,768]{4,3,2,1,0:T(8,128)(2,1)}), bf16[256,1,1,12,768]{4,3,2,1,0:T(8,128)(2,1)}, u32[]{:S(2)}, u32[]{:S(2)}) %all-to-all-start.1) | async-done | bytes 4718624 | tf_op jit(solution)/shard_map/all_to_all | solution.py:25
  234.7 8.4 %reshape_reshape.4 = bf16[3072,768]{1,0:T(8,128)(2,1)} reshape(bf16[8,32,1,12,768]{4,3,1,0,2:T(8,128)(2,1)} %bitcast.12) | data formatting | bytes 9437184 | tf_op jit(solution)/shard_map/reshape;reshape | solution.py:96
  243.0 0.0 copy-done.4
  243.0 5.3 %fusion.12 = f32[256,768]{1,0:T(8,128)} fusion(bf16[3072,768]{1,0:T(8,128)(2,1)} %reshape_reshape.4, s32[3072]{0:T(1024)S(1)} %select_n.39, f32[256]{0:T(256)S(1)} %maximum_convert_fusion), kind=kOutput, calls=%fused_computation.22 | convolution fusion | flops 1208942592 | bytes 5518336 | tf_op jit(solution)/shard_map/dot_general | solution.py:52
  (12 shorter events, 0.1 us)
Async XLA Ops:
  0.6 57.2 %copy-start = (bf16[1024,768]{1,0:T(8,128)(2,1)S(1)}, bf16[1024,768]{1,0:T(8,128)(2,1)}, u32[]{:S(2)}) copy-start(bf16[1024,768]{1,0:T(8,128)(2,1)} %param.8) | copy-start | bytes 4718596
  0.6 1.7 copy-start.3
  0.7 22.5 %copy-start.2 = (s32[1024,64]{0,1:T(8,128)S(1)}, s32[1024,64]{0,1:T(8,128)}, u32[]{:S(2)}) copy-start(s32[1024,64]{0,1:T(8,128)} %param.9) | copy-start | bytes 786436
  0.7 23.3 %copy-start.1 = (bf16[256,768]{1,0:T(8,128)(2,1)S(1)}, bf16[256,768]{1,0:T(8,128)(2,1)}, u32[]{:S(2)}) copy-start(bf16[256,768]{1,0:T(8,128)(2,1)} %param.12) | copy-start | bytes 1179652
  7.5 70.5 %all-to-all-start = ((s32[256,1,1,12]{3,2,1,0:T(1,128)}), s32[256,1,1,12]{3,2,1,0:T(1,128)S(1)}, u32[]{:S(2)}, u32[]{:S(2)}) async-start(s32[256,1,1,12]{3,2,1,0:T(1,128)} %bitcast.2), calls=%async_computation | async-start | bytes 262144 | tf_op jit(solution)/shard_map/all_to_all | solution.py:25
  78.0 16.3 %copy-start.5 = (s32[256]{0:T(256)S(1)}, s32[256]{0:T(256)}, u32[]{:S(2)}) copy-start(s32[256]{0:T(256)} %param.13) | copy-start | bytes 3076
  78.0 156.7 %all-to-all-start.1 = ((bf16[256,1,1,12,768]{4,3,2,1,0:T(8,128)(2,1)}), bf16[256,1,1,12,768]{4,3,2,1,0:T(8,128)(2,1)}, u32[]{:S(2)}, u32[]{:S(2)}) async-start(bf16[256,1,1,12,768]{4,3,2,1,0:T(8,128)(2,1)} %bitcast.47), calls=%async_computation.1 | async-start | bytes 12582912 | tf_op jit(solution)/shard_map/all_to_all | solution.py:25
  94.9 148.2 %copy-start.4 = (s32[256]{0:T(256)}, s32[256]{0:T(256)S(1)}, u32[]{:S(2)}) copy-start(s32[256]{0:T(256)S(1)} %get-tuple-element.47) | copy-start | bytes 3076
where the time goes:
time: 250 us; the launch traced here: 248 us
  waiting for transfers between devices  140 us (56%)
  local copies, waits for them, and re-layouts  41.3 us (17%)
  matrix products  33.2 us (13%)
  starting transfers between devices  30.2 us (12%)
  other arithmetic  2.96 us (1%)
    all_to_all x2, waiting for transfers between devices, one_exchange(): lax.all_to_all(blocks, axis, split_axis=0, concat_axis=0, tiled=True)  140 us
    all_to_all x2, starting transfers between devices, one_exchange(): lax.all_to_all(blocks, axis, split_axis=0, concat_axis=0, tiled=True)  30.2 us
    dot_general x4, matrix products, one_block(): jnp.einsum('bmk,kmj->bmj', picker, code_table, preferred_element_type=jnp...  23.5 us
    another operation x2, local copies, waits for them, and re-layouts, one_exchange(): blocks = blocks.reshape(-1, *inside)  9.05 us
    another operation x1, local copies, waits for them, and re-layouts, local(): got_rows = got_rows.reshape(-1, feat_width)  8.37 us
    scatter x1, local copies, waits for them, and re-layouts, local(): send_rows = jnp.zeros((owner_total * slot_cap, feat_width), jnp.bfloat16)...  8.23 us
    dot_general x1, matrix products, sum_by_list(): lax.dot_general(picker, rows_in, (((0,), (0,)), ((), ())), preferred_elem...  5.29 us
  transfers between devices with their start and end apart: 2, of which 1 were waited for; matrix products, arithmetic and copies ran while one was open for 23% of the time, Pallas kernels for 0%

commit v1 on v0

v1 whole, which is shorter than its diff:
```python
import functools

import jax
import jax.numpy as jnp
from jax import lax
from jax.experimental import pallas as pl
from jax.experimental.pallas import tpu as pltpu
from jax.sharding import PartitionSpec as P

MESH = pl.DeviceIdType.MESH
D = 768
M = 64
DSUB = 12
KSUB = 256
VEC = 1024
LISTS = 256
PEERS = 32
ZS = 8
F32 = jnp.float32
BF = jnp.bfloat16

_RING = (
    [(1, 2), (2, 1), (3, 2), (2, 3), (2, 2)]
    + [(1, 1), (3, 3), (1, 3), (3, 1)]
    + [(2, 0), (0, 2)]
    + [(1, 0), (0, 1), (3, 0), (0, 3)]
)
ORDER = [(a, b, 0) for a, b in _RING] + [(a, b, 1) for a, b in _RING] + [(0, 0, 1)]


def coords():
    row = lax.axis_index("row")
    col = lax.axis_index("col")
    return (row // 4) * 2 + col // 16, row % 4, (col // 2) % 8, col % 2


def device(x, y, z, c):
    return ((x // 2) * 4 + y, (x % 2) * 16 + z * 2 + c)


def encode_kernel(cap, group, chunks, me_ref, res_ref, codes_ref, ids_ref, rot_ref, book_ref,
                  slots_ref, tags_ref, table_ref, built_ref, err_ref):
    width = D // chunks
    lanes = cap * group
    ids = ids_ref[...]
    owner = ids // LISTS
    inner = ids % LISTS
    col = owner % 32
    row = owner // 32
    zed = (col // 2) % 8
    spot = (((row // 4) * 2 + col // 16) * 4 + row % 4) * 2 + col % 2
    at_peer = (lax.broadcasted_iota(jnp.int32, (PEERS, VEC), 0) == spot).astype(F32)

    blocks = jnp.concatenate([at_peer[:, b * 128:(b + 1) * 128] for b in range(VEC // 128)], axis=0).astype(BF)
    before = (lax.broadcasted_iota(jnp.int32, (128, 128), 0) < lax.broadcasted_iota(jnp.int32, (128, 128), 1)).astype(BF)
    inside = jnp.dot(blocks, before, preferred_element_type=F32)
    whole = jnp.dot(blocks, jnp.ones((128, 128), BF), preferred_element_type=F32)
    offset = jnp.zeros((PEERS, 128), F32)
    ranks = []
    for b in range(VEC // 128):
        part = inside[b * PEERS:(b + 1) * PEERS] + offset
        ranks.append(jnp.sum(part * at_peer[:, b * 128:(b + 1) * 128], axis=0, keepdims=True))
        offset = offset + whole[b * PEERS:(b + 1) * PEERS]
    rank = jnp.concatenate(ranks, axis=1).astype(jnp.int32)
    slot = spot * cap + rank

    lane = rank + cap * (me_ref[0] % group)
    lane_hot = (lax.broadcasted_iota(jnp.int32, (lanes, VEC), 0) == lane).astype(F32).astype(BF)
    tag_rows = jnp.concatenate([at_peer * (zed + 1).astype(F32), at_peer * inner.astype(F32)], axis=0).astype(BF)
    found = lax.dot_general(tag_rows, lane_hot, (((1,), (1,)), ((), ())), preferred_element_type=F32)
    tags = (found[:PEERS] - 1.0) * LISTS + found[PEERS:]
    tags_ref[...] = tags.astype(jnp.int32).reshape(PEERS, 1, lanes)

    line = lax.broadcasted_iota(jnp.int32, (D, D), 0)
    feature = (line % M) * DSUB + line // M
    perm = (lax.broadcasted_iota(jnp.int32, (D, D), 1) == feature).astype(F32).astype(BF)
    table_ref[...] = lax.dot_general(perm, book_ref[...], (((1,), (1,)), ((), ())), preferred_element_type=F32)
    codes = codes_ref[...]
    for j in range(DSUB):
        low = table_ref[j * M:(j + 1) * M, :128]
        high = table_ref[j * M:(j + 1) * M, 128:]
        for b in range(VEC // 128):
            index = codes[:, b * 128:(b + 1) * 128]
            near = index % 128
            picked = jnp.where(
                index < 128,
                jnp.take_along_axis(low, near, axis=1, mode="promise_in_bounds"),
                jnp.take_along_axis(high, near, axis=1, mode="promise_in_bounds"),
            )
            built_ref[j * M:(j + 1) * M, b * 128:(b + 1) * 128] = picked.astype(BF)
    rebuilt = lax.dot_general(built_ref[...], perm, (((0,), (0,)), ((), ())), preferred_element_type=F32)
    rotated = jnp.dot(res_ref[...], rot_ref[...], preferred_element_type=F32)
    err_ref[...] = (rotated - rebuilt).astype(BF)

    rows = 256

    def place(i, _):
        start = pl.multiple_of(i * rows, rows)
        pick = (lax.broadcasted_iota(jnp.int32, (rows, VEC), 0) + start == slot).astype(F32).astype(BF)
        for k in range(chunks):
            moved = jnp.dot(pick, err_ref[:, k * width:(k + 1) * width], preferred_element_type=F32)
            slots_ref[k, pl.ds(start, rows), :] = moved.astype(BF)
        return 0

    lax.fori_loop(0, PEERS * cap // rows, place, 0)


def encode(cap, group, chunks, me, residuals, codes, ids, rotation, codebook):
    vmem = pl.BlockSpec(memory_space=pltpu.VMEM)
    return pl.pallas_call(
        functools.partial(encode_kernel, cap, group, chunks),
        out_shape=(
            jax.ShapeDtypeStruct((chunks, PEERS * cap, D // chunks), BF),
            jax.ShapeDtypeStruct((PEERS, 1, cap * group), jnp.int32),
        ),
        in_specs=[pl.BlockSpec(memory_space=pltpu.SMEM)] + [vmem] * 5,
        out_specs=(vmem, vmem),
        scratch_shapes=[
            pltpu.VMEM((D, KSUB), F32),
            pltpu.VMEM((D, VEC), BF),
            pltpu.VMEM((VEC, D), BF),
        ],
        compiler_params=pltpu.CompilerParams(vmem_limit_bytes=50 * 2**20),
    )(me, residuals, codes, ids, rotation, codebook)


def exchange_kernel(cap, group, chunks, slots_ref, tags_ref, sums_ref, counts_ref,
                    rows, tag_in, hot, part, z_out, z_in, cnt_out, cnt_in,
                    row_ssem, row_rsem, own_sem, tag_ssem, tag_rsem, tag_own,
                    z_ssem, z_rsem, cnt_ssem, cnt_rsem):
    x, y, z, c = coords()
    me = (x * 4 + y) * 2 + c
    width = D // chunks
    half = width // 2
    lanes = cap * group

    barrier = pltpu.get_barrier_semaphore()
    for dx, dy, dc in ORDER:
        pl.semaphore_signal(barrier, inc=1, device_id=device((x + dx) % 4, (y + dy) % 4, z, (c + dc) % 2), device_id_type=MESH)
    for dz in range(1, ZS):
        pl.semaphore_signal(barrier, inc=1, device_id=device(x, y, (z + dz) % 8, c), device_id_type=MESH)
    pl.semaphore_wait(barrier, len(ORDER) + ZS - 1)

    def peer(o):
        dx, dy, dc = o
        px, py, pc = (x + dx) % 4, (y + dy) % 4, (c + dc) % 2
        return (px * 4 + py) * 2 + pc, device(px, py, z, pc)

    def tag_copy(k):
        spot, dev = peer(ORDER[k])
        return pltpu.make_async_remote_copy(
            tags_ref.at[spot], tag_in.at[me], tag_ssem.at[k], tag_rsem.at[k], device_id=dev, device_id_type=MESH)

    def row_copy(ch, k):
        spot, dev = peer(ORDER[k])
        return pltpu.make_async_remote_copy(
            slots_ref.at[ch, pl.ds(pl.multiple_of(spot * cap, 16), cap)],
            rows.at[ch, pl.ds(pl.multiple_of(me * cap, 16), cap)],
            row_ssem.at[ch, k], row_rsem.at[ch, k], device_id=dev, device_id_type=MESH)

    def own_copy(ch):
        span = pl.ds(pl.multiple_of(me * cap, 16), cap)
        return pltpu.make_async_copy(slots_ref.at[ch, span], rows.at[ch, span], own_sem.at[ch])

    def tag_keep():
        return pltpu.make_async_copy(tags_ref.at[me], tag_in.at[me], tag_own)

    for k in range(len(ORDER)):
        tag_copy(k).start()
    tag_keep().start()

    def start_rows(ch, _):
        for k in range(len(ORDER)):
            row_copy(ch, k).start()
        own_copy(ch).start()
        return 0

    lax.fori_loop(0, chunks, start_rows, 0)

    for k in range(len(ORDER)):
        tag_copy(k).wait()
    tag_keep().wait()

    eye = (lax.broadcasted_iota(jnp.int32, (128, 128), 0) == lax.broadcasted_iota(jnp.int32, (128, 128), 1)).astype(F32)

    def make_hot(d, _):
        names = lax.broadcasted_iota(jnp.int32, (LISTS, 128), 0) + d * LISTS
        total = jnp.zeros((LISTS, 128), F32)
        for q in range(PEERS // group):
            tag = tag_in[q * group]
            for i in range(1, group):
                tag = jnp.maximum(tag, tag_in[q * group + i])
            for j in range(lanes // 128):
                one = (names == tag[:, j * 128:(j + 1) * 128]).astype(F32)
                total = total + one
                hot[d, :, q * lanes + j * 128:q * lanes + (j + 1) * 128] = one.astype(BF)
        spread = jnp.dot(total.astype(BF), jnp.ones((128, 128), BF), preferred_element_type=F32)
        for b in range(LISTS // 128):
            cnt_out[d, :, b * 128:(b + 1) * 128] = jnp.sum(spread[b * 128:(b + 1) * 128] * eye, axis=0, keepdims=True)
        return 0

    lax.fori_loop(0, ZS, make_hot, 0)

    def cnt_copy(dz):
        to = (z + dz) % 8
        return pltpu.make_async_remote_copy(
            cnt_out.at[to], cnt_in.at[z], cnt_ssem.at[dz], cnt_rsem.at[dz],
            device_id=device(x, y, to, c), device_id_type=MESH)

    for dz in range(1, ZS):
        cnt_copy(dz).start()

    def length(h, s):
        return 4 if h == s else 3

    def z_copy(ch, h, s, t):
        to = (z + (1 if s == 0 else 7)) % 8
        return pltpu.make_async_remote_copy(
            z_out.at[ch, h, s, t], z_in.at[ch, h, s, t], z_ssem.at[ch, h, s, t], z_rsem.at[ch, h, s, t],
            device_id=device(x, y, to, c), device_id_type=MESH)

    def finish(ch, _):
        for k in range(len(ORDER)):
            row_copy(ch, k).wait()
        own_copy(ch).wait()

        def table(d):
            return jnp.dot(hot[d], rows[ch], preferred_element_type=F32)

        far = table((z + 4) % 8)
        for h in (0, 1):
            z_out[ch, h, h, 0] = far[:, h * half:(h + 1) * half].astype(BF)
            z_copy(ch, h, h, 0).start()
        for s in (0, 1):
            near = table((z + (3 if s == 0 else 5)) % 8)
            part[3, s] = near
            h = 1 - s
            z_out[ch, h, s, 0] = near[:, h * half:(h + 1) * half].astype(BF)
            z_copy(ch, h, s, 0).start()
        for k in (2, 1):
            for s in (0, 1):
                part[k, s] = table((z + (k if s == 0 else 8 - k)) % 8)
        part[0, 0] = table(z)
        for k in (3, 2, 1):
            for s in (0, 1):
                for h in (0, 1):
                    t = length(h, s) - k
                    if t > 0:
                        z_copy(ch, h, s, t - 1).wait_recv()
                        own = part[k, s, :, h * half:(h + 1) * half]
                        z_out[ch, h, s, t] = (own + z_in[ch, h, s, t - 1].astype(F32)).astype(BF)
                        z_copy(ch, h, s, t).start()
        for h in (0, 1):
            total = part[0, 0, :, h * half:(h + 1) * half]
            for s in (0, 1):
                last = length(h, s) - 1
                z_copy(ch, h, s, last).wait_recv()
                total = total + z_in[ch, h, s, last].astype(F32)
            sums_ref[ch, h] = total
        return 0

    lax.fori_loop(0, chunks, finish, 0)

    def drain(ch, _):
        for h in (0, 1):
            for s in (0, 1):
                for t in range(length(h, s)):
                    z_copy(ch, h, s, t).wait_send()
        return 0

    lax.fori_loop(0, chunks, drain, 0)

    total = cnt_out[z]
    for dz in range(1, ZS):
        cnt_copy(dz).wait()
        total = total + cnt_in[(z + 8 - dz) % 8]
    counts_ref[...] = total


def exchange(cap, group, chunks, slots, tags):
    vmem = pl.BlockSpec(memory_space=pltpu.VMEM)
    width = D // chunks
    half = width // 2
    n = len(ORDER)
    lanes = cap * group
    dma = pltpu.SemaphoreType.DMA
    return pl.pallas_call(
        functools.partial(exchange_kernel, cap, group, chunks),
        out_shape=(
            jax.ShapeDtypeStruct((chunks, 2, LISTS, half), F32),
            jax.ShapeDtypeStruct((1, LISTS), F32),
        ),
        in_specs=[pl.BlockSpec(memory_space=pl.ANY), vmem],
        out_specs=(vmem, vmem),
        scratch_shapes=[
            pltpu.VMEM((chunks, PEERS * cap, width), BF),
            pltpu.VMEM((PEERS, 1, lanes), jnp.int32),
            pltpu.VMEM((ZS, LISTS, PEERS * cap), BF),
            pltpu.VMEM((4, 2, LISTS, width), F32),
            pltpu.VMEM((chunks, 2, 2, 4, LISTS, half), BF),
            pltpu.VMEM((chunks, 2, 2, 4, LISTS, half), BF),
            pltpu.VMEM((ZS, 1, LISTS), F32),
            pltpu.VMEM((ZS, 1, LISTS), F32),
            dma((chunks, n)), dma((chunks, n)), dma((chunks,)),
            dma((n,)), dma((n,)), dma,
            dma((chunks, 2, 2, 4)), dma((chunks, 2, 2, 4)),
            dma((ZS,)), dma((ZS,)),
        ],
        compiler_params=pltpu.CompilerParams(
            collective_id=0, has_side_effects=True, vmem_limit_bytes=60 * 2**20),
    )(slots, tags)


def local(residuals, codes, list_ids, rotation, codebook, list_fill):
    x, y, z, c = coords()
    me = ((x * 4 + y) * 2 + c).reshape(1)
    cap, group, chunks = 96, 4, 3
    slots, tags = encode(cap, group, chunks, me, residuals, codes.T, list_ids.reshape(1, VEC), rotation, codebook)
    sums, counts = exchange(cap, group, chunks, slots, tags)
    list_counts = counts.reshape(LISTS).astype(jnp.int32)
    divisor = jnp.maximum(list_counts, 1).astype(F32)
    sums = jnp.transpose(sums.reshape(chunks * 2, LISTS, D // chunks // 2), (1, 0, 2)).reshape(LISTS, D)
    list_drift = sums / divisor[:, None]
    new_blocks = (list_fill + list_counts + 127) // 128 - (list_fill + 127) // 128
    return list_drift, list_counts, new_blocks


def solution(mesh):
    split = P(("row", "col"))
    wide = P(("row", "col"), None)
    return jax.shard_map(
        local,
        mesh=mesh,
        in_specs=(wide, wide, split, P(), P(), split),
        out_specs=(wide, split, split),
        check_vma=False,
    )
```

time: 250 us -> 119 us (0.48)
  the two profiles are of different devices: /device:TPU:1 before, /device:TPU:2 now
where the time goes in v1:
time: 119 us; the launch traced here: 117 us
  Pallas kernels  107 us (90%)
  local copies, waits for them, and re-layouts  8.49 us (7%)
    pallas_call x1, Pallas kernels, exchange(): pl.pallas_call(functools.partial(exchange_kernel, cap, group, chunks), ou...  91.2 us
    pallas_call x1, Pallas kernels, encode(): pl.pallas_call(functools.partial(encode_kernel, cap, group, chunks), out_...  15.6 us
    unnamed x19, local copies, waits for them, and re-layouts  7.09 us

profile of v1, /device:TPU:2, one launch (start us, length us, event | category | flops | bytes accessed | tf_op | source)
XLA Modules:
  0.0 116.7 jit_solution(15080386076322080022)
XLA Ops:
  0.7 0.0 copy-start
  0.7 1.4 %copy-done = bf16[1024,768]{1,0:T(8,128)(2,1)S(1)} copy-done((bf16[1024,768]{1,0:T(8,128)(2,1)S(1)}, bf16[1024,768]{1,0:T(8,128)(2,1)}, u32[]{:S(2)}) %copy-start) | copy-done | bytes 1572888
  2.1 0.0 copy-start.1
  2.1 1.3 %copy-done.1 = bf16[768,768]{1,0:T(8,128)(2,1)S(1)} copy-done((bf16[768,768]{1,0:T(8,128)(2,1)S(1)}, bf16[768,768]{1,0:T(8,128)(2,1)}, u32[]{:S(2)}) %copy-start.1) | copy-done | bytes 1179672
  3.4 0.0 copy-start.2
  3.4 1.0 copy-done.2
  4.3 0.0 copy-start.3
  4.4 0.9 copy-done.3
  5.3 0.0 copy-start.5
  5.3 0.7 copy-done.5
  6.0 15.6 %shard_map.85 = (bf16[3,3072,256]{2,1,0:T(8,128)(2,1)}, s32[32,1,384]{2,1,0:T(1,128)S(1)}) custom-call(s32[1]{0:T(128)} %bitcast.me_ref, bf16[1024,768]{1,0:T(8,128)(2,1)S(1)} %copy-done, s32[64,1024]{1,0:T(8,128)S(1)} %bitcast.9, s32[1,1024]{1,0:T(1,128)S(1)} %bitcast.10, bf16[768,768]{1,0:T(8,128)(2,1)S(1)} %copy-done.1, bf16[256,768]{1,0:T(8,128)(2,1)S(1)} %copy-done.2), custom_call_target="tpu_custom_call" | custom-call | tf_op jit(solution)/shard_map/pallas_call | solution.py:110
  21.6 0.0 copy-start.4
  21.6 0.6 copy-done.4
  22.2 91.2 %shard_map.86 = (f32[3,2,256,128]{3,2,1,0:T(8,128)}, f32[1,256]{1,0:T(1,128)}) custom-call(bf16[3,3072,256]{2,1,0:T(8,128)(2,1)} %get-tuple-element.7.slots_ref, s32[32,1,384]{2,1,0:T(1,128)} %copy-done.4), custom_call_target="tpu_custom_call" | custom-call | tf_op jit(solution)/shard_map/pallas_call | solution.py:287
  113.4 0.0 copy-start.7
  113.4 0.0 copy-start.8
  113.4 1.4 %copy.10 = f32[6,256,128]{1,2,0:T(8,128)S(1)} copy(f32[6,256,128]{2,1,0:T(8,128)} %bitcast.11) | data formatting | bytes 1572864 | tf_op jit(solution)/shard_map/reshape | solution.py:322
  114.9 0.0 copy-done.7
  114.9 0.0 copy-start.6
  114.9 0.0 copy-done.8
  114.9 0.6 fusion
  115.5 0.1 bitcast_divide_fusion
  115.5 1.1 copy.11
  116.7 0.0 copy-done.6
  (1 shorter events, 0.0 us)
Async XLA Ops:
  0.7 1.4 %copy-start = (bf16[1024,768]{1,0:T(8,128)(2,1)S(1)}, bf16[1024,768]{1,0:T(8,128)(2,1)}, u32[]{:S(2)}) copy-start(bf16[1024,768]{1,0:T(8,128)(2,1)} %res_ref.1) | copy-start | bytes 4718596
  2.1 1.3 %copy-start.1 = (bf16[768,768]{1,0:T(8,128)(2,1)S(1)}, bf16[768,768]{1,0:T(8,128)(2,1)}, u32[]{:S(2)}) copy-start(bf16[768,768]{1,0:T(8,128)(2,1)} %rot_ref.1) | copy-start | bytes 3538948
  3.4 1.0 copy-start.2
  4.3 0.9 copy-start.3
  5.3 0.7 copy-start.5
  21.6 0.6 copy-start.4
  113.4 1.4 %copy-start.7 = (f32[1,256]{1,0:T(1,128)S(1)}, f32[1,256]{1,0:T(1,128)}, u32[]{:S(2)}) copy-start(f32[1,256]{1,0:T(1,128)} %get-tuple-element.10) | copy-start | bytes 3076
  113.4 1.5 %copy-start.8 = (s32[256]{0:T(256)S(1)}, s32[256]{0:T(256)}, u32[]{:S(2)}) copy-start(s32[256]{0:T(256)} %param.11) | copy-start | bytes 3076
  114.9 1.8 %copy-start.6 = (s32[1,256]{1,0:T(1,128)}, s32[1,256]{1,0:T(1,128)S(1)}, u32[]{:S(2)}) copy-start(s32[1,256]{1,0:T(1,128)S(1)} %convert_element_type.17) | copy-start | bytes 3076

commit v2 on v1

v2 whole, which is shorter than its diff:
```python
import functools

import jax
import jax.numpy as jnp
from jax import lax
from jax.experimental import pallas as pl
from jax.experimental.pallas import tpu as pltpu
from jax.sharding import PartitionSpec as P

MESH = pl.DeviceIdType.MESH
D = 768
M = 64
DSUB = 12
KSUB = 256
VEC = 1024
LISTS = 256
PEERS = 32
ZS = 8
CHUNKS = 6
WIDTH = D // CHUNKS
HALF = LISTS // 2
F32 = jnp.float32
BF = jnp.bfloat16

_RING = (
    [(1, 2), (2, 1), (3, 2), (2, 3), (2, 2)]
    + [(1, 1), (3, 3), (1, 3), (3, 1)]
    + [(2, 0), (0, 2)]
    + [(1, 0), (0, 1), (3, 0), (0, 3)]
)
ORDER = [(a, b, 0) for a, b in _RING] + [(a, b, 1) for a, b in _RING] + [(0, 0, 1)]


def coords():
    row = lax.axis_index("row")
    col = lax.axis_index("col")
    return (row // 4) * 2 + col // 16, row % 4, (col // 2) % 8, col % 2


def device(x, y, z, c):
    return ((x // 2) * 4 + y, (x % 2) * 16 + z * 2 + c)


def greet(barrier, x, y, z, c):
    for dx, dy, dc in ORDER:
        pl.semaphore_signal(barrier, inc=1, device_id=device((x + dx) % 4, (y + dy) % 4, z, (c + dc) % 2), device_id_type=MESH)
    for dz in range(1, ZS):
        pl.semaphore_signal(barrier, inc=1, device_id=device(x, y, (z + dz) % 8, c), device_id_type=MESH)


def one_hot(names, index, start, size):
    shifted = index - start
    inside = jnp.logical_and(shifted >= 0, shifted < size)
    row = jnp.where(inside, shifted, -1).astype(F32).astype(BF)
    return jnp.where(names == row, jnp.ones((), BF), jnp.zeros((), BF))


def encode_kernel(res_hbm, codes_hbm, ids_ref, rot_hbm, book_hbm, err_ref, plan_ref, most_ref,
                  res_ref, codes_ref, rot_ref, book_ref, table_ref, built_ref,
                  here_out, here_in, all_out, all_in, sems, here_ssem, here_rsem, all_ssem, all_rsem):
    x, y, z, c = coords()
    barrier = pltpu.get_barrier_semaphore()
    greet(barrier, x, y, z, c)
    loads = [
        pltpu.make_async_copy(src, dst, sems.at[i])
        for i, (src, dst) in enumerate(
            [(book_hbm, book_ref), (codes_hbm, codes_ref), (res_hbm, res_ref), (rot_hbm, rot_ref)])
    ]
    for load in loads:
        load.start()

    ids = ids_ref[...]
    owner = ids // LISTS
    inner = ids % LISTS
    col = owner % 32
    row = owner // 32
    zed = (col // 2) % 8
    spot = (((row // 4) * 2 + col // 16) * 4 + row % 4) * 2 + col % 2
    at_peer = (lax.broadcasted_iota(jnp.int32, (PEERS, VEC), 0) == spot).astype(F32)
    blocks = jnp.concatenate([at_peer[:, b * 128:(b + 1) * 128] for b in range(VEC // 128)], axis=0).astype(BF)
    before = (lax.broadcasted_iota(jnp.int32, (128, 128), 0) < lax.broadcasted_iota(jnp.int32, (128, 128), 1)).astype(F32).astype(BF)
    inside = jnp.dot(blocks, before, preferred_element_type=F32)
    whole = jnp.dot(blocks, jnp.ones((128, 128), BF), preferred_element_type=F32)
    offset = jnp.zeros((PEERS, 128), F32)
    for b in range(VEC // 128):
        part = inside[b * PEERS:(b + 1) * PEERS] + offset
        rank = jnp.sum(part * at_peer[:, b * 128:(b + 1) * 128], axis=0, keepdims=True)
        plan_ref[1:2, b * 128:(b + 1) * 128] = rank.astype(jnp.int32)
        offset = offset + whole[b * PEERS:(b + 1) * PEERS]
    here_out[...] = jnp.max(offset, axis=0, keepdims=True)
    pl.semaphore_wait(barrier, len(ORDER) + ZS - 1)
    for k, (dx, dy, dc) in enumerate(ORDER):
        pltpu.make_async_remote_copy(
            here_out, here_in.at[k], here_ssem, here_rsem,
            device_id=device((x + dx) % 4, (y + dy) % 4, z, (c + dc) % 2), device_id_type=MESH).start()
    plan_ref[0:1, :] = spot
    plan_ref[2:3, :] = zed
    plan_ref[3:4, :] = inner
    plan_ref[4:8, :] = jnp.zeros((4, VEC), jnp.int32)

    line = lax.broadcasted_iota(jnp.int32, (D, D), 0)
    feature = (line % M) * DSUB + line // M
    perm = (lax.broadcasted_iota(jnp.int32, (D, D), 1) == feature).astype(F32).astype(BF)
    for load in loads:
        load.wait()
    table_ref[...] = lax.dot_general(perm, book_ref[...], (((1,), (1,)), ((), ())), preferred_element_type=F32)
    codes = codes_ref[...]
    for j in range(DSUB):
        low = table_ref[j * M:(j + 1) * M, :128]
        high = table_ref[j * M:(j + 1) * M, 128:]
        for b in range(VEC // 128):
            index = codes[:, b * 128:(b + 1) * 128]
            near = index % 128
            picked = jnp.where(
                index < 128,
                jnp.take_along_axis(low, near, axis=1, mode="promise_in_bounds"),
                jnp.take_along_axis(high, near, axis=1, mode="promise_in_bounds"),
            )
            built_ref[j * M:(j + 1) * M, b * 128:(b + 1) * 128] = picked.astype(BF)
    pltpu.make_async_copy(here_in, here_in, here_rsem).wait()
    most = here_out[...]
    for k in range(len(ORDER)):
        most = jnp.maximum(most, here_in[k])
    all_out[...] = most
    for dz in range(1, ZS):
        pltpu.make_async_remote_copy(
            all_out, all_in.at[dz - 1], all_ssem, all_rsem,
            device_id=device(x, y, (z + dz) % 8, c), device_id_type=MESH).start()
    rebuilt = lax.dot_general(built_ref[...], perm, (((0,), (0,)), ((), ())), preferred_element_type=F32)
    rotated = jnp.dot(res_ref[...], rot_ref[...], preferred_element_type=F32)
    error = (rotated - rebuilt).astype(BF)
    for k in range(CHUNKS):
        err_ref[k] = error[:, k * WIDTH:(k + 1) * WIDTH]
    pltpu.make_async_copy(all_in, all_in, all_rsem).wait()
    for i in range(ZS - 1):
        most = jnp.maximum(most, all_in[i])
    most_ref[...] = most.astype(jnp.int32)
    pltpu.make_async_copy(here_in, here_in, here_ssem).wait()
    pltpu.make_async_copy(all_in, all_in, all_ssem).wait()


def encode(residuals, codes, ids, rotation, codebook):
    vmem = pl.BlockSpec(memory_space=pltpu.VMEM)
    hbm = pl.BlockSpec(memory_space=pltpu.HBM)
    return pl.pallas_call(
        encode_kernel,
        out_shape=(
            jax.ShapeDtypeStruct((CHUNKS, VEC, WIDTH), BF),
            jax.ShapeDtypeStruct((8, VEC), jnp.int32),
            jax.ShapeDtypeStruct((1, 128), jnp.int32),
        ),
        in_specs=[hbm, hbm, vmem, hbm, hbm],
        out_specs=(vmem, vmem, vmem),
        scratch_shapes=[
            pltpu.VMEM((VEC, D), BF),
            pltpu.VMEM((M, VEC), jnp.int32),
            pltpu.VMEM((D, D), BF),
            pltpu.VMEM((KSUB, D), BF),
            pltpu.VMEM((D, KSUB), F32),
            pltpu.VMEM((D, VEC), BF),
            pltpu.VMEM((1, 128), F32),
            pltpu.VMEM((PEERS - 1, 1, 128), F32),
            pltpu.VMEM((1, 128), F32),
            pltpu.VMEM((ZS - 1, 1, 128), F32),
            pltpu.SemaphoreType.DMA((4,)),
            pltpu.SemaphoreType.DMA, pltpu.SemaphoreType.DMA,
            pltpu.SemaphoreType.DMA, pltpu.SemaphoreType.DMA,
        ],
        compiler_params=pltpu.CompilerParams(
            collective_id=0, has_side_effects=True, vmem_limit_bytes=63 * 2**20),
    )(residuals, codes, ids, rotation, codebook)


def exchange_kernel(cap, group, err_ref, plan_ref, sums_ref, counts_ref,
                    pick, slots, rows, tag_out, tag_in, hot, part, z_out, z_in, cnt_out, cnt_in,
                    row_ssem, row_rsem, tag_ssem, tag_rsem,
                    z_ssem, z_rsem, cnt_ssem, cnt_rsem):
    x, y, z, c = coords()
    me = (x * 4 + y) * 2 + c
    lanes = cap * group
    total_slots = PEERS * cap

    barrier = pltpu.get_barrier_semaphore()
    greet(barrier, x, y, z, c)

    def peer(o):
        dx, dy, dc = o
        px, py, pc = (x + dx) % 4, (y + dy) % 4, (c + dc) % 2
        return (px * 4 + py) * 2 + pc, device(px, py, z, pc)

    def tag_copy(k):
        spot, dev = peer(ORDER[k])
        return pltpu.make_async_remote_copy(
            tag_out.at[spot], tag_in.at[me], tag_ssem, tag_rsem, device_id=dev, device_id_type=MESH)

    def row_copy(ch, k):
        spot, dev = peer(ORDER[k])
        return pltpu.make_async_remote_copy(
            slots.at[ch, pl.ds(pl.multiple_of(spot * cap, 16), cap)],
            rows.at[ch, pl.ds(pl.multiple_of(me * cap, 16), cap)],
            row_ssem.at[ch], row_rsem.at[ch], device_id=dev, device_id_type=MESH)

    def own_copy(ch):
        span = pl.ds(pl.multiple_of(me * cap, 16), cap)
        return pltpu.make_async_copy(slots.at[ch, span], rows.at[ch, span], row_rsem.at[ch])

    def tag_keep():
        return pltpu.make_async_copy(tag_out.at[me], tag_in.at[me], tag_rsem)

    spot = plan_ref[0:1, :]
    rank = plan_ref[1:2, :]
    at_peer = (lax.broadcasted_iota(jnp.int32, (PEERS, VEC), 0) == spot).astype(F32)
    lane = rank + cap * (me % group)
    wide_names = lax.broadcasted_iota(jnp.int32, (LISTS, VEC), 0).astype(F32).astype(BF)
    lane_hot = jnp.concatenate([one_hot(wide_names[:128], lane, j * 128, 128) for j in range(lanes // 128)], axis=0)
    tag_rows = jnp.concatenate(
        [at_peer * (plan_ref[2:3, :] + 1).astype(F32), at_peer * plan_ref[3:4, :].astype(F32)], axis=0).astype(BF)
    found = lax.dot_general(tag_rows, lane_hot, (((1,), (1,)), ((), ())), preferred_element_type=F32)
    tags = (found[:PEERS] - 1.0) * LISTS + found[PEERS:]
    tag_out[...] = tags.astype(jnp.int32).reshape(PEERS, 1, lanes)

    slot = spot * cap + rank

    def place_first(i, _):
        start = pl.multiple_of(i * 256, 256)
        one = one_hot(wide_names, slot, start, 256)
        pick[pl.ds(start, 256), :] = one
        slots[0, pl.ds(start, 256), :] = jnp.dot(one, err_ref[0], preferred_element_type=F32).astype(BF)
        return 0

    def place(ch):
        def one(i, _):
            start = pl.multiple_of(i * 512, 512)
            slots[ch, pl.ds(start, 512), :] = jnp.dot(
                pick[pl.ds(start, 512), :], err_ref[ch], preferred_element_type=F32).astype(BF)
            return 0

        lax.fori_loop(0, total_slots // 512, one, 0)

    def send(ch):
        for k in range(len(ORDER)):
            row_copy(ch, k).start()
        own_copy(ch).start()

    lax.fori_loop(0, total_slots // 256, place_first, 0)
    pl.semaphore_wait(barrier, len(ORDER) + ZS - 1)
    for k in range(len(ORDER)):
        tag_copy(k).start()
    tag_keep().start()
    send(0)
    place(1)
    send(1)

    pltpu.make_async_copy(tag_in, tag_in, tag_rsem).wait()
    others = pl.ds(0, PEERS - 1)
    pltpu.make_async_copy(tag_out.at[others], tag_out.at[others], tag_ssem).wait()

    eye = (lax.broadcasted_iota(jnp.int32, (128, 128), 0) == lax.broadcasted_iota(jnp.int32, (128, 128), 1)).astype(F32)

    names = lax.broadcasted_iota(jnp.int32, (LISTS, 128), 0).astype(F32).astype(BF)
    tag = []
    for q in range(PEERS // group):
        joined = tag_in[q * group]
        for i in range(1, group):
            joined = jnp.maximum(joined, tag_in[q * group + i])
        tag += [joined[:, j * 128:(j + 1) * 128] for j in range(lanes // 128)]

    def make_hot(d, _):
        total = jnp.zeros((LISTS, 128), BF)
        for j in range(total_slots // 128):
            one = one_hot(names, tag[j], d * LISTS, LISTS)
            total = total + one
            hot[d, :, j * 128:(j + 1) * 128] = one
        spread = jnp.dot(total, jnp.ones((128, 128), BF), preferred_element_type=F32)
        for b in range(LISTS // 128):
            cnt_out[d, :, b * 128:(b + 1) * 128] = jnp.sum(spread[b * 128:(b + 1) * 128] * eye, axis=0, keepdims=True)
        return 0

    lax.fori_loop(0, ZS, make_hot, 0)

    def cnt_copy(dz):
        to = (z + dz) % 8
        return pltpu.make_async_remote_copy(
            cnt_out.at[to], cnt_in.at[z], cnt_ssem.at[dz], cnt_rsem.at[dz],
            device_id=device(x, y, to, c), device_id_type=MESH)

    for dz in range(1, ZS):
        cnt_copy(dz).start()

    def length(h, s):
        return 4 if h == s else 3

    def z_copy(ch, h, s, t):
        to = (z + (1 if s == 0 else 7)) % 8
        return pltpu.make_async_remote_copy(
            z_out.at[ch, h, s, t], z_in.at[ch, h, s, t], z_ssem.at[ch], z_rsem.at[ch, h, s, t],
            device_id=device(x, y, to, c), device_id_type=MESH)

    def table(ch, d):
        return jnp.dot(hot[d], rows[ch], preferred_element_type=F32)

    def reduce(ch):
        pltpu.make_async_copy(rows.at[ch], rows.at[ch], row_rsem.at[ch]).wait()
        flip = ch % 2
        far = table(ch, (z + 4) % 8)
        for h in (0, 1):
            z_out[ch, h, h, 0] = far[h * HALF:(h + 1) * HALF].astype(BF)
            z_copy(ch, h, h, 0).start()
        for s in (0, 1):
            near = table(ch, (z + (3 if s == 0 else 5)) % 8)
            part[flip, 3, s] = near
            h = 1 - s
            z_out[ch, h, s, 0] = near[h * HALF:(h + 1) * HALF].astype(BF)
            z_copy(ch, h, s, 0).start()
        for k in (2, 1):
            for s in (0, 1):
                part[flip, k, s] = table(ch, (z + (k if s == 0 else 8 - k)) % 8)
        part[flip, 0, 0] = table(ch, z)

    def hop(ch, k):
        flip = ch % 2
        for h in (0, 1):
            for s in (0, 1):
                t = length(h, s) - k
                if t > 0:
                    z_copy(ch, h, s, t - 1).wait_recv()
                    own = part[flip, k, s, h * HALF:(h + 1) * HALF]
                    z_out[ch, h, s, t] = (own + z_in[ch, h, s, t - 1].astype(F32)).astype(BF)
                    z_copy(ch, h, s, t).start()

    def settle(ch):
        flip = ch % 2
        for h in (0, 1):
            total = part[flip, 0, 0, h * HALF:(h + 1) * HALF]
            for s in (0, 1):
                last = length(h, s) - 1
                z_copy(ch, h, s, last).wait_recv()
                total = total + z_in[ch, h, s, last].astype(F32)
            sums_ref[h * HALF:(h + 1) * HALF, pl.ds(pl.multiple_of(ch * WIDTH, WIDTH), WIDTH)] = total

    def round_trip(ch, _):
        reduce(ch)

        @pl.when(ch > 0)
        def _():
            hop(ch - 1, 1)

        hop(ch, 3)

        @pl.when(ch + 2 < CHUNKS)
        def _():
            place(ch + 2)
            send(ch + 2)

        @pl.when(ch > 0)
        def _():
            settle(ch - 1)

        hop(ch, 2)
        return 0

    lax.fori_loop(0, CHUNKS, round_trip, 0)
    hop(CHUNKS - 1, 1)
    settle(CHUNKS - 1)

    def drain(ch, _):
        others = slots.at[ch, pl.ds(0, (PEERS - 1) * cap)]
        pltpu.make_async_copy(others, others, row_ssem.at[ch]).wait()
        first = z_out.at[ch, 0]
        rest = z_out.at[ch, 1, pl.ds(0, 1)]
        pltpu.make_async_copy(first, first, z_ssem.at[ch]).wait()
        pltpu.make_async_copy(rest, rest, z_ssem.at[ch]).wait()
        tip = z_out.at[ch, 1, 1, pl.ds(0, 2)]
        pltpu.make_async_copy(tip, tip, z_ssem.at[ch]).wait()
        return 0

    lax.fori_loop(0, CHUNKS, drain, 0)

    total = cnt_out[z]
    for dz in range(1, ZS):
        cnt_copy(dz).wait()
        total = total + cnt_in[(z + 8 - dz) % 8]
    counts_ref[...] = total


def exchange(cap, group, number, err, plan):
    vmem = pl.BlockSpec(memory_space=pltpu.VMEM)
    lanes = cap * group
    dma = pltpu.SemaphoreType.DMA
    return pl.pallas_call(
        functools.partial(exchange_kernel, cap, group),
        out_shape=(
            jax.ShapeDtypeStruct((LISTS, D), F32),
            jax.ShapeDtypeStruct((1, LISTS), F32),
        ),
        in_specs=[vmem, vmem],
        out_specs=(vmem, vmem),
        scratch_shapes=[
            pltpu.VMEM((PEERS * cap, VEC), BF),
            pltpu.VMEM((CHUNKS, PEERS * cap, WIDTH), BF),
            pltpu.VMEM((CHUNKS, PEERS * cap, WIDTH), BF),
            pltpu.VMEM((PEERS, 1, lanes), jnp.int32),
            pltpu.VMEM((PEERS, 1, lanes), jnp.int32),
            pltpu.VMEM((ZS, LISTS, PEERS * cap), BF),
            pltpu.VMEM((2, 4, 2, LISTS, WIDTH), F32),
            pltpu.VMEM((CHUNKS, 2, 2, 4, HALF, WIDTH), BF),
            pltpu.VMEM((CHUNKS, 2, 2, 4, HALF, WIDTH), BF),
            pltpu.VMEM((ZS, 1, LISTS), F32),
            pltpu.VMEM((ZS, 1, LISTS), F32),
            dma((CHUNKS,)), dma((CHUNKS,)), dma, dma,
            dma((CHUNKS,)), dma((CHUNKS, 2, 2, 4)),
            dma((ZS,)), dma((ZS,)),
        ],
        compiler_params=pltpu.CompilerParams(
            collective_id=number, has_side_effects=True, vmem_limit_bytes=63 * 2**20),
    )(err, plan)


def local(residuals, codes, list_ids, rotation, codebook, list_fill):
    err, plan, most = encode(residuals, codes.T, list_ids.reshape(1, VEC), rotation, codebook)
    sums, counts = lax.cond(
        most[0, 0] <= 64,
        functools.partial(exchange, 64, 2, 1),
        functools.partial(exchange, 96, 4, 2),
        err, plan)
    list_counts = counts.reshape(LISTS).astype(jnp.int32)
    divisor = jnp.maximum(list_counts, 1).astype(F32)
    list_drift = sums / divisor[:, None]
    new_blocks = (list_fill + list_counts + 127) // 128 - (list_fill + 127) // 128
    return list_drift, list_counts, new_blocks


def solution(mesh):
    split = P(("row", "col"))
    wide = P(("row", "col"), None)
    return jax.shard_map(
        local,
        mesh=mesh,
        in_specs=(wide, wide, split, P(), P(), split),
        out_specs=(wide, split, split),
        check_vma=False,
    )
```

time: 119 us -> 92.7 us (0.78); the launches traced: 117 us -> 92.5 us
  Pallas kernels: 107 us -> 88.5 us
  local copies, waits for them, and re-layouts: 8.49 us -> 0.01 us
  other arithmetic: 0.64 us -> 2.25 us
    pallas_call x2, Pallas kernels: 107 us -> 88.5 us  [the longest x1 69.2 us: exchange(): pl.pallas_call(functools.partial(exchange_kernel, cap, group), out_shape=...]
    unnamed x19 -> x4, local copies, waits for them, and re-layouts: 7.09 us -> 0.01 us
    reshape x1 -> x0, local copies, waits for them, and re-layouts: 1.4 us -> none  [local(): sums.reshape(chunks * 2, LISTS, D // chunks // 2)]
where the time goes in v2:
time: 92.7 us; the launch traced here: 92.5 us
  Pallas kernels  88.5 us (95%)
  other arithmetic  2.25 us (2%)
  between operations  1.29 us (1%)
    pallas_call x1, Pallas kernels, exchange(): pl.pallas_call(functools.partial(exchange_kernel, cap, group), out_shape=...  69.2 us
    pallas_call x1, Pallas kernels, encode(): pl.pallas_call(encode_kernel, out_shape=(jax.ShapeDtypeStruct((CHUNKS, VE...  19.3 us

profile of v2, /device:TPU:2, one launch (start us, length us, event | category | flops | bytes accessed | tf_op | source)
XLA Modules:
  0.0 92.5 jit_solution(718632276982546936)
XLA Ops:
  0.6 19.3 %shard_map.85 = (bf16[6,1024,128]{2,1,0:T(8,128)(2,1)}, s32[8,1024]{1,0:T(8,128)S(1)}, s32[1,128]{1,0:T(1,128)}) custom-call(bf16[1024,768]{1,0:T(8,128)(2,1)} %res_hbm.1, s32[64,1024]{1,0:T(8,128)} %bitcast.6, s32[1,1024]{1,0:T(1,128)} %bitcast.7, bf16[768,768]{1,0:T(8,128)(2,1)} %rot_hbm.1, bf16[256,768]{1,0:T(8,128)(2,1)} %book_hbm.1), custom_call_target="tpu_custom_call" | custom-call | tf_op jit(solution)/shard_map/pallas_call | solution.py:145
  20.6 0.0 copy-start.1
  20.6 70.3 %conditional.1 = (f32[256,768]{1,0:T(8,128)S(1)}, s32[256]{0:T(256)S(1)}) conditional(s32[]{:T(128)} %bitcast.2, (bf16[6,1024,128]{2,1,0:T(8,128)(2,1)}, s32[8,1024]{1,0:T(8,128)S(1)}) %tuple.29, (bf16[6,1024,128]{2,1,0:T(8,128)(2,1)}, s32[8,1024]{1,0:T(8,128)S(1)}) %tuple.29), branch_computations={%region_0.0_spmd.clone, %region_1.0_spmd.clone} | conditional | flops 256 | bytes 2064 | solution.py:421
  21.0 69.2 %branch_1_fun.3 = (f32[256,768]{1,0:T(8,128)S(1)}, f32[1,256]{1,0:T(1,128)}) custom-call(bf16[6,1024,128]{2,1,0:T(8,128)(2,1)} %get-tuple-element.63.err_ref, s32[8,1024]{1,0:T(8,128)S(1)} %get-tuple-element.64.plan_ref), custom_call_target="tpu_custom_call" | custom-call | tf_op jit(solution)/shard_map/cond/branch_1_fun/pallas_call | solution.py:390
  90.2 0.7 convert_element_type.44
  90.9 0.0 copy-start
  90.9 0.0 copy-done.1
  90.9 0.6 fusion
  91.5 1.0 %broadcast_divide_fusion = f32[256,768]{1,0:T(8,128)} fusion(f32[256,768]{1,0:T(8,128)S(1)} %get-tuple-element.55, f32[256]{0:T(256)S(1)} %get-tuple-element.75), kind=kLoop, calls=%fused_computation | loop fusion | flops 196608 | bytes 1573888 | tf_op jit(solution)/shard_map/div | solution.py:428
  92.5 0.0 copy-done
Async XLA Ops:
  20.6 70.3 %copy-start.1 = (s32[256]{0:T(256)S(1)}, s32[256]{0:T(256)}, u32[]{:S(2)}) copy-start(s32[256]{0:T(256)} %param.13) | copy-start | bytes 3076
  90.9 1.6 %copy-start = (s32[256]{0:T(256)}, s32[256]{0:T(256)S(1)}, u32[]{:S(2)}) copy-start(s32[256]{0:T(256)S(1)} %get-tuple-element.73) | copy-start | bytes 3076

commit v3 on v2

v3 whole, which is shorter than its diff:
```python
import functools

import jax
import jax.numpy as jnp
from jax import lax
from jax.experimental import pallas as pl
from jax.experimental.pallas import tpu as pltpu
from jax.sharding import PartitionSpec as P

MESH = pl.DeviceIdType.MESH
D = 768
M = 64
DSUB = 12
KSUB = 256
VEC = 1024
LISTS = 256
PEERS = 32
ZS = 8
CHUNKS = 6
WIDTH = D // CHUNKS
HALF = LISTS // 2
CAP = 64
REST = 32
F32 = jnp.float32
BF = jnp.bfloat16

_RING = (
    [(1, 2), (2, 1), (3, 2), (2, 3), (2, 2)]
    + [(1, 1), (3, 3), (1, 3), (3, 1)]
    + [(2, 0), (0, 2)]
    + [(1, 0), (0, 1), (3, 0), (0, 3)]
)
ORDER = [(a, b, 0) for a, b in _RING] + [(a, b, 1) for a, b in _RING] + [(0, 0, 1)]


def coords():
    row = lax.axis_index("row")
    col = lax.axis_index("col")
    return (row // 4) * 2 + col // 16, row % 4, (col // 2) % 8, col % 2


def device(x, y, z, c):
    return ((x // 2) * 4 + y, (x % 2) * 16 + z * 2 + c)


def greet(barrier, x, y, z, c):
    for dx, dy, dc in ORDER:
        pl.semaphore_signal(barrier, inc=1, device_id=device((x + dx) % 4, (y + dy) % 4, z, (c + dc) % 2), device_id_type=MESH)
    for dz in range(1, ZS):
        pl.semaphore_signal(barrier, inc=1, device_id=device(x, y, (z + dz) % 8, c), device_id_type=MESH)


def one_hot(names, index, start, size):
    shifted = index - start
    inside = jnp.logical_and(shifted >= 0, shifted < size)
    row = jnp.where(inside, shifted, -1).astype(F32).astype(BF)
    return jnp.where(names == row, jnp.ones((), BF), jnp.zeros((), BF))


def window_kernel(cap, group, base, res_hbm, codes_hbm, ids_ref, rot_hbm, book_hbm,
                  sums_ref, counts_ref, most_ref,
                  pair, weights, codes_ref, book_ref, table_ref, err, here_out, here_in, all_out, all_in,
                  pick, slots, rows, tag_out, tag_in, hot, part, z_out, z_in, cnt_out, cnt_in,
                  load_sem, here_ssem, here_rsem, all_ssem, all_rsem,
                  row_ssem, row_rsem, tag_ssem, tag_rsem, z_ssem, z_rsem, cnt_ssem, cnt_rsem):
    x, y, z, c = coords()
    me = (x * 4 + y) * 2 + c
    lanes = cap * group
    total_slots = PEERS * cap

    barrier = pltpu.get_barrier_semaphore()
    greet(barrier, x, y, z, c)
    loads = [
        pltpu.make_async_copy(src, dst, load_sem.at[i])
        for i, (src, dst) in enumerate([
            (book_hbm, book_ref), (codes_hbm, codes_ref),
            (res_hbm, pair.at[:, pl.ds(0, D)]), (rot_hbm, weights.at[pl.ds(0, D)])])
    ]
    for load in loads:
        load.start()

    ids = ids_ref[...]
    owner = ids // LISTS
    inner = ids % LISTS
    col = owner % 32
    row = owner // 32
    zed = (col // 2) % 8
    spot = (((row // 4) * 2 + col // 16) * 4 + row % 4) * 2 + col % 2
    at_peer = (lax.broadcasted_iota(jnp.int32, (PEERS, VEC), 0) == spot).astype(F32)
    blocks = jnp.concatenate([at_peer[:, b * 128:(b + 1) * 128] for b in range(VEC // 128)], axis=0).astype(BF)
    before = (lax.broadcasted_iota(jnp.int32, (128, 128), 0) < lax.broadcasted_iota(jnp.int32, (128, 128), 1)).astype(F32).astype(BF)
    inside = jnp.dot(blocks, before, preferred_element_type=F32)
    whole = jnp.dot(blocks, jnp.ones((128, 128), BF), preferred_element_type=F32)
    offset = jnp.zeros((PEERS, 128), F32)
    ranks = []
    for b in range(VEC // 128):
        ranks.append(jnp.sum((inside[b * PEERS:(b + 1) * PEERS] + offset) * at_peer[:, b * 128:(b + 1) * 128], axis=0, keepdims=True))
        offset = offset + whole[b * PEERS:(b + 1) * PEERS]
    rank = jnp.concatenate(ranks, axis=1).astype(jnp.int32) - base
    here_out[...] = jnp.max(offset, axis=0, keepdims=True)
    fits = jnp.logical_and(rank >= 0, rank < cap)
    slot = jnp.where(fits, spot * cap + rank, -1)
    lane = jnp.where(fits, rank + cap * (me % group), -1)

    wide_names = lax.broadcasted_iota(jnp.int32, (LISTS, VEC), 0).astype(F32).astype(BF)
    lane_hot = jnp.concatenate([one_hot(wide_names[:128], lane, j * 128, 128) for j in range(lanes // 128)], axis=0)
    tag_rows = jnp.concatenate([at_peer * (zed + 1).astype(F32), at_peer * inner.astype(F32)], axis=0).astype(BF)
    found = lax.dot_general(tag_rows, lane_hot, (((1,), (1,)), ((), ())), preferred_element_type=F32)
    tags = (found[:PEERS] - 1.0) * LISTS + found[PEERS:]
    tag_out[...] = tags.astype(jnp.int32).reshape(PEERS, 1, lanes)

    line = lax.broadcasted_iota(jnp.int32, (D, D), 0)
    feature = (line % M) * DSUB + line // M
    perm = (lax.broadcasted_iota(jnp.int32, (D, D), 1) == feature).astype(F32).astype(BF)
    weights[D:, :] = perm
    for load in loads[:2]:
        load.wait()
    table_ref[...] = -lax.dot_general(perm, book_ref[...], (((1,), (1,)), ((), ())), preferred_element_type=F32)
    for b in range(VEC // 128):
        index = codes_ref[:, b * 128:(b + 1) * 128]
        index = jnp.concatenate([index, index], axis=0)
        near = index % 128
        for j in range(D // 128):
            picked = jnp.where(
                index < 128,
                jnp.take_along_axis(table_ref[j * 128:(j + 1) * 128, :128], near, axis=1, mode="promise_in_bounds"),
                jnp.take_along_axis(table_ref[j * 128:(j + 1) * 128, 128:], near, axis=1, mode="promise_in_bounds"),
            )
            pair[b * 128:(b + 1) * 128, D + j * 128:D + (j + 1) * 128] = picked.T.astype(BF)
    for load in loads[2:]:
        load.wait()

    def encode(p):
        error = jnp.dot(pair[...], weights[:, 2 * p * WIDTH:2 * (p + 1) * WIDTH], preferred_element_type=F32).astype(BF)
        err[2 * p] = error[:, :WIDTH]
        err[2 * p + 1] = error[:, WIDTH:]

    def peer(o):
        dx, dy, dc = o
        px, py, pc = (x + dx) % 4, (y + dy) % 4, (c + dc) % 2
        return (px * 4 + py) * 2 + pc, device(px, py, z, pc)

    def tag_copy(k):
        spot, dev = peer(ORDER[k])
        return pltpu.make_async_remote_copy(
            tag_out.at[spot], tag_in.at[me], tag_ssem, tag_rsem, device_id=dev, device_id_type=MESH)

    def row_copy(ch, k):
        spot, dev = peer(ORDER[k])
        return pltpu.make_async_remote_copy(
            slots.at[ch, pl.ds(pl.multiple_of(spot * cap, 16), cap)],
            rows.at[ch, pl.ds(pl.multiple_of(me * cap, 16), cap)],
            row_ssem.at[ch], row_rsem.at[ch], device_id=dev, device_id_type=MESH)

    def own_copy(ch):
        span = pl.ds(pl.multiple_of(me * cap, 16), cap)
        return pltpu.make_async_copy(slots.at[ch, span], rows.at[ch, span], row_rsem.at[ch])

    def tag_keep():
        return pltpu.make_async_copy(tag_out.at[me], tag_in.at[me], tag_rsem)

    def place_first(i, _):
        start = pl.multiple_of(i * 256, 256)
        one = one_hot(wide_names, slot, start, 256)
        pick[pl.ds(start, 256), :] = one
        slots[0, pl.ds(start, 256), :] = jnp.dot(one, err[0], preferred_element_type=F32).astype(BF)
        return 0

    def place(ch):
        def one(i, _):
            start = pl.multiple_of(i * 512, 512)
            slots[ch, pl.ds(start, 512), :] = jnp.dot(
                pick[pl.ds(start, 512), :], err[ch], preferred_element_type=F32).astype(BF)
            return 0

        lax.fori_loop(0, total_slots // 512, one, 0)

    def send(ch):
        for k in range(len(ORDER)):
            row_copy(ch, k).start()
        own_copy(ch).start()

    encode(0)
    lax.fori_loop(0, total_slots // 256, place_first, 0)
    pl.semaphore_wait(barrier, len(ORDER) + ZS - 1)
    for k in range(len(ORDER)):
        tag_copy(k).start()
    tag_keep().start()
    send(0)
    for k in range(len(ORDER)):
        pltpu.make_async_remote_copy(
            here_out, here_in.at[k], here_ssem, here_rsem, device_id=peer(ORDER[k])[1], device_id_type=MESH).start()
    place(1)
    send(1)
    encode(1)
    encode(2)

    pltpu.make_async_copy(tag_in, tag_in, tag_rsem).wait()
    others = pl.ds(0, PEERS - 1)
    pltpu.make_async_copy(tag_out.at[others], tag_out.at[others], tag_ssem).wait()

    eye = (lax.broadcasted_iota(jnp.int32, (128, 128), 0) == lax.broadcasted_iota(jnp.int32, (128, 128), 1)).astype(F32)
    names = lax.broadcasted_iota(jnp.int32, (LISTS, 128), 0).astype(F32).astype(BF)
    tag = []
    for q in range(PEERS // group):
        joined = tag_in[q * group]
        for i in range(1, group):
            joined = jnp.maximum(joined, tag_in[q * group + i])
        tag += [joined[:, j * 128:(j + 1) * 128] for j in range(lanes // 128)]

    def make_hot(d, _):
        total = jnp.zeros((LISTS, 128), BF)
        for j in range(total_slots // 128):
            one = one_hot(names, tag[j], d * LISTS, LISTS)
            total = total + one
            hot[d, :, j * 128:(j + 1) * 128] = one
        spread = jnp.dot(total, jnp.ones((128, 128), BF), preferred_element_type=F32)
        for b in range(LISTS // 128):
            cnt_out[d, :, b * 128:(b + 1) * 128] = jnp.sum(spread[b * 128:(b + 1) * 128] * eye, axis=0, keepdims=True)
        return 0

    lax.fori_loop(0, ZS, make_hot, 0)

    def cnt_copy(dz):
        to = (z + dz) % 8
        return pltpu.make_async_remote_copy(
            cnt_out.at[to], cnt_in.at[z], cnt_ssem.at[dz], cnt_rsem.at[dz],
            device_id=device(x, y, to, c), device_id_type=MESH)

    pltpu.make_async_copy(here_in, here_in, here_rsem).wait()
    most = here_out[...]
    for k in range(len(ORDER)):
        most = jnp.maximum(most, here_in[k])
    all_out[...] = most
    for dz in range(1, ZS):
        cnt_copy(dz).start()
        pltpu.make_async_remote_copy(
            all_out, all_in.at[dz - 1], all_ssem, all_rsem,
            device_id=device(x, y, (z + dz) % 8, c), device_id_type=MESH).start()

    def length(h, s):
        return 4 if h == s else 3

    def z_copy(ch, h, s, t):
        to = (z + (1 if s == 0 else 7)) % 8
        return pltpu.make_async_remote_copy(
            z_out.at[ch, h, s, t], z_in.at[ch, h, s, t], z_ssem.at[ch], z_rsem.at[ch, h, s, t],
            device_id=device(x, y, to, c), device_id_type=MESH)

    def table(ch, d):
        return jnp.dot(hot[d], rows[ch], preferred_element_type=F32)

    def reduce(ch):
        pltpu.make_async_copy(rows.at[ch], rows.at[ch], row_rsem.at[ch]).wait()
        turn = ch % 3
        far = table(ch, (z + 4) % 8)
        for h in (0, 1):
            z_out[ch, h, h, 0] = far[h * HALF:(h + 1) * HALF].astype(BF)
            z_copy(ch, h, h, 0).start()
        for s in (0, 1):
            near = table(ch, (z + (3 if s == 0 else 5)) % 8)
            part[turn, 3, s] = near
            h = 1 - s
            z_out[ch, h, s, 0] = near[h * HALF:(h + 1) * HALF].astype(BF)
            z_copy(ch, h, s, 0).start()
        for k in (2, 1):
            for s in (0, 1):
                part[turn, k, s] = table(ch, (z + (k if s == 0 else 8 - k)) % 8)
        part[turn, 0, 0] = table(ch, z)

    def hop(ch, k):
        turn = ch % 3
        for h in (0, 1):
            for s in (0, 1):
                t = length(h, s) - k
                if t > 0:
                    z_copy(ch, h, s, t - 1).wait_recv()
                    own = part[turn, k, s, h * HALF:(h + 1) * HALF]
                    z_out[ch, h, s, t] = (own + z_in[ch, h, s, t - 1].astype(F32)).astype(BF)
                    z_copy(ch, h, s, t).start()

    def settle(ch):
        turn = ch % 3
        for h in (0, 1):
            total = part[turn, 0, 0, h * HALF:(h + 1) * HALF]
            for s in (0, 1):
                last = length(h, s) - 1
                z_copy(ch, h, s, last).wait_recv()
                total = total + z_in[ch, h, s, last].astype(F32)
            sums_ref[h * HALF:(h + 1) * HALF, pl.ds(pl.multiple_of(ch * WIDTH, WIDTH), WIDTH)] = total

    def period(ch, _):
        reduce(ch)

        @pl.when(ch > 1)
        def _():
            hop(ch - 2, 1)

        @pl.when(ch > 0)
        def _():
            hop(ch - 1, 2)

        @pl.when(ch + 2 < CHUNKS)
        def _():
            place(ch + 2)
            send(ch + 2)

        hop(ch, 3)

        @pl.when(ch > 1)
        def _():
            settle(ch - 2)

        return 0

    lax.fori_loop(0, CHUNKS, period, 0)
    hop(CHUNKS - 2, 1)
    hop(CHUNKS - 1, 2)
    settle(CHUNKS - 2)
    hop(CHUNKS - 1, 1)

    pltpu.make_async_copy(all_in, all_in, all_rsem).wait()
    for i in range(ZS - 1):
        most = jnp.maximum(most, all_in[i])
    most_ref[...] = most.astype(jnp.int32)
    total = cnt_out[z]
    for dz in range(1, ZS):
        cnt_copy(dz).wait()
        total = total + cnt_in[(z + 8 - dz) % 8]
    counts_ref[...] = total.astype(jnp.int32)
    pltpu.make_async_copy(here_in, here_in, here_ssem).wait()
    pltpu.make_async_copy(all_in, all_in, all_ssem).wait()

    def drain(ch, _):
        sent = slots.at[ch, pl.ds(0, (PEERS - 1) * cap)]
        pltpu.make_async_copy(sent, sent, row_ssem.at[ch]).wait()
        for piece in (z_out.at[ch, 0], z_out.at[ch, 1, pl.ds(0, 1)], z_out.at[ch, 1, 1, pl.ds(0, 2)]):
            pltpu.make_async_copy(piece, piece, z_ssem.at[ch]).wait()
        return 0

    lax.fori_loop(0, CHUNKS, drain, 0)
    settle(CHUNKS - 1)


def window(cap, group, base, number, residuals, codes, ids, rotation, codebook):
    vmem = pl.BlockSpec(memory_space=pltpu.VMEM)
    hbm = pl.BlockSpec(memory_space=pltpu.HBM)
    lanes = cap * group
    dma = pltpu.SemaphoreType.DMA
    return pl.pallas_call(
        functools.partial(window_kernel, cap, group, base),
        out_shape=(
            jax.ShapeDtypeStruct((LISTS, D), F32),
            jax.ShapeDtypeStruct((1, LISTS), jnp.int32),
            jax.ShapeDtypeStruct((1, 128), jnp.int32),
        ),
        in_specs=[hbm, hbm, vmem, hbm, hbm],
        out_specs=(vmem, vmem, vmem),
        scratch_shapes=[
            pltpu.VMEM((VEC, 2 * D), BF),
            pltpu.VMEM((2 * D, D), BF),
            pltpu.VMEM((M, VEC), jnp.int32),
            pltpu.VMEM((KSUB, D), BF),
            pltpu.VMEM((D, KSUB), F32),
            pltpu.VMEM((CHUNKS, VEC, WIDTH), BF),
            pltpu.VMEM((1, 128), F32),
            pltpu.VMEM((PEERS - 1, 1, 128), F32),
            pltpu.VMEM((1, 128), F32),
            pltpu.VMEM((ZS - 1, 1, 128), F32),
            pltpu.VMEM((PEERS * cap, VEC), BF),
            pltpu.VMEM((CHUNKS, PEERS * cap, WIDTH), BF),
            pltpu.VMEM((CHUNKS, PEERS * cap, WIDTH), BF),
            pltpu.VMEM((PEERS, 1, lanes), jnp.int32),
            pltpu.VMEM((PEERS, 1, lanes), jnp.int32),
            pltpu.VMEM((ZS, LISTS, PEERS * cap), BF),
            pltpu.VMEM((3, 4, 2, LISTS, WIDTH), F32),
            pltpu.VMEM((CHUNKS, 2, 2, 4, HALF, WIDTH), BF),
            pltpu.VMEM((CHUNKS, 2, 2, 4, HALF, WIDTH), BF),
            pltpu.VMEM((ZS, 1, LISTS), F32),
            pltpu.VMEM((ZS, 1, LISTS), F32),
            dma((4,)), dma, dma, dma, dma,
            dma((CHUNKS,)), dma((CHUNKS,)), dma, dma,
            dma((CHUNKS,)), dma((CHUNKS, 2, 2, 4)),
            dma((ZS,)), dma((ZS,)),
        ],
        compiler_params=pltpu.CompilerParams(
            collective_id=number, has_side_effects=True, vmem_limit_bytes=63 * 2**20),
    )(residuals, codes, ids, rotation, codebook)


def local(residuals, codes, list_ids, rotation, codebook, list_fill):
    given = (residuals, codes.T, list_ids.reshape(1, VEC), rotation, codebook)
    sums, counts, most = window(CAP, 2, 0, 0, *given)

    def rest(sums, counts, *given):
        more, extra, _ = window(REST, 4, CAP, 1, *given)
        return sums + more, counts + extra

    def done(sums, counts, *given):
        return sums, counts

    sums, counts = lax.cond(most[0, 0] > CAP, rest, done, sums, counts, *given)
    list_counts = counts.reshape(LISTS)
    divisor = jnp.maximum(list_counts, 1).astype(F32)
    list_drift = sums / divisor[:, None]
    new_blocks = (list_fill + list_counts + 127) // 128 - (list_fill + 127) // 128
    return list_drift, list_counts, new_blocks


def solution(mesh):
    split = P(("row", "col"))
    wide = P(("row", "col"), None)
    return jax.shard_map(
        local,
        mesh=mesh,
        in_specs=(wide, wide, split, P(), P(), split),
        out_specs=(wide, split, split),
        check_vma=False,
    )
```

time: 92.7 us -> 82.3 us (0.89)
  Pallas kernels: 88.5 us -> 77.3 us
  local copies, waits for them, and re-layouts: 0.01 us -> 1.05 us
    pallas_call x2 -> x1, Pallas kernels: 88.5 us -> 77.3 us  [window(): pl.pallas_call(functools.partial(window_kernel, cap, group, base), out_sh...]
    unnamed x4 -> x5, local copies, waits for them, and re-layouts: 0.01 us -> 1.05 us
where the time goes in v3:
time: 82.3 us; the launch traced here: 81.4 us
  Pallas kernels  77.3 us (94%)
  other arithmetic  1.58 us (2%)
  between operations  1.35 us (2%)
  local copies, waits for them, and re-layouts  1.05 us (1%)
    pallas_call x1, Pallas kernels, window(): pl.pallas_call(functools.partial(window_kernel, cap, group, base), out_sh...  77.3 us

profile of v3, /device:TPU:2, one launch (start us, length us, event | category | flops | bytes accessed | tf_op | source)
XLA Modules:
  0.0 81.4 jit_solution(9414683989204179401)
XLA Ops:
  0.6 0.0 copy-start
  0.6 77.3 %shard_map.85 = (f32[256,768]{1,0:T(8,128)S(1)}, s32[1,256]{1,0:T(1,128)S(1)}, s32[1,128]{1,0:T(1,128)}) custom-call(bf16[1024,768]{1,0:T(8,128)(2,1)} %res_hbm.1, s32[64,1024]{1,0:T(8,128)} %bitcast.5, s32[1,1024]{1,0:T(1,128)} %bitcast.7, bf16[768,768]{1,0:T(8,128)(2,1)} %rot_hbm.1, bf16[256,768]{1,0:T(8,128)(2,1)} %book_hbm.1), custom_call_target="tpu_custom_call" | custom-call | tf_op jit(solution)/shard_map/pallas_call | solution.py:350
  78.6 0.0 copy-done
  78.6 0.0 copy-start.2
  78.6 0.2 conditional.1
  78.8 0.5 copy-done.2
  79.3 0.6 fusion
  79.9 1.0 %broadcast_divide_fusion = f32[256,768]{1,0:T(8,128)} fusion(f32[256,768]{1,0:T(8,128)S(1)} %get-tuple-element.64, f32[256]{0:T(256)S(1)} %get-tuple-element.67), kind=kLoop, calls=%fused_computation | loop fusion | flops 196608 | bytes 1573888 | tf_op jit(solution)/shard_map/div | solution.py:405
  80.9 0.6 copy.14
Async XLA Ops:
  0.6 78.0 %copy-start = (s32[1024]{0:T(1024)S(1)}, s32[1024]{0:T(1024)}, u32[]{:S(2)}) copy-start(s32[1024]{0:T(1024)} %param.10) | copy-start | bytes 12292
  78.6 0.7 copy-start.2

commit v4 on v3

--- a/solution.py
+++ b/solution.py
@@ -180,16 +180,16 @@
             row_copy(ch, k).start()
         own_copy(ch).start()
 
-    encode(0)
-    lax.fori_loop(0, total_slots // 256, place_first, 0)
     pl.semaphore_wait(barrier, len(ORDER) + ZS - 1)
     for k in range(len(ORDER)):
         tag_copy(k).start()
     tag_keep().start()
-    send(0)
     for k in range(len(ORDER)):
         pltpu.make_async_remote_copy(
             here_out, here_in.at[k], here_ssem, here_rsem, device_id=peer(ORDER[k])[1], device_id_type=MESH).start()
+    encode(0)
+    lax.fori_loop(0, total_slots // 256, place_first, 0)
+    send(0)
     place(1)
     send(1)
     encode(1)
@@ -252,7 +252,7 @@
 
     def reduce(ch):
         pltpu.make_async_copy(rows.at[ch], rows.at[ch], row_rsem.at[ch]).wait()
-        turn = ch % 3
+        turn = ch % 5
         far = table(ch, (z + 4) % 8)
         for h in (0, 1):
             z_out[ch, h, h, 0] = far[h * HALF:(h + 1) * HALF].astype(BF)
@@ -269,7 +269,7 @@
         part[turn, 0, 0] = table(ch, z)
 
     def hop(ch, k):
-        turn = ch % 3
+        turn = ch % 5
         for h in (0, 1):
             for s in (0, 1):
                 t = length(h, s) - k
@@ -280,7 +280,7 @@
                     z_copy(ch, h, s, t).start()
 
     def settle(ch):
-        turn = ch % 3
+        turn = ch % 5
         for h in (0, 1):
             total = part[turn, 0, 0, h * HALF:(h + 1) * HALF]
             for s in (0, 1):
@@ -289,57 +289,69 @@
                 total = total + z_in[ch, h, s, last].astype(F32)
             sums_ref[h * HALF:(h + 1) * HALF, pl.ds(pl.multiple_of(ch * WIDTH, WIDTH), WIDTH)] = total
 
+    def count():
+        total = cnt_out[z]
+        for dz in range(1, ZS):
+            cnt_copy(dz).wait()
+            total = total + cnt_in[(z + 8 - dz) % 8]
+        counts_ref[...] = total.astype(jnp.int32)
+        pltpu.make_async_copy(all_in, all_in, all_rsem).wait()
+        top = all_out[...]
+        for i in range(ZS - 1):
+            top = jnp.maximum(top, all_in[i])
+        most_ref[...] = top.astype(jnp.int32)
+
     def period(ch, _):
         reduce(ch)
 
-        @pl.when(ch > 1)
+        @pl.when(ch >= 2)
         def _():
             hop(ch - 2, 1)
 
-        @pl.when(ch > 0)
+        @pl.when(ch >= 1)
         def _():
             hop(ch - 1, 2)
+
+        @pl.when(ch >= 3)
+        def _():
+            settle(ch - 3)
 
         @pl.when(ch + 2 < CHUNKS)
         def _():
             place(ch + 2)
             send(ch + 2)
 
+        @pl.when(ch == 1)
+        def _():
+            count()
+
         hop(ch, 3)
-
-        @pl.when(ch > 1)
-        def _():
-            settle(ch - 2)
-
         return 0
 
     lax.fori_loop(0, CHUNKS, period, 0)
     hop(CHUNKS - 2, 1)
     hop(CHUNKS - 1, 2)
+    settle(CHUNKS - 3)
     settle(CHUNKS - 2)
     hop(CHUNKS - 1, 1)
 
-    pltpu.make_async_copy(all_in, all_in, all_rsem).wait()
-    for i in range(ZS - 1):
-        most = jnp.maximum(most, all_in[i])
-    most_ref[...] = most.astype(jnp.int32)
-    total = cnt_out[z]
-    for dz in range(1, ZS):
-        cnt_copy(dz).wait()
-        total = total + cnt_in[(z + 8 - dz) % 8]
-    counts_ref[...] = total.astype(jnp.int32)
     pltpu.make_async_copy(here_in, here_in, here_ssem).wait()
     pltpu.make_async_copy(all_in, all_in, all_ssem).wait()
 
     def drain(ch, _):
         sent = slots.at[ch, pl.ds(0, (PEERS - 1) * cap)]
         pltpu.make_async_copy(sent, sent, row_ssem.at[ch]).wait()
+        return 0
+
+    lax.fori_loop(0, CHUNKS, drain, 0)
+    settle(CHUNKS - 1)
+
+    def drain_z(ch, _):
         for piece in (z_out.at[ch, 0], z_out.at[ch, 1, pl.ds(0, 1)], z_out.at[ch, 1, 1, pl.ds(0, 2)]):
             pltpu.make_async_copy(piece, piece, z_ssem.at[ch]).wait()
         return 0
 
-    lax.fori_loop(0, CHUNKS, drain, 0)
-    settle(CHUNKS - 1)
+    lax.fori_loop(0, CHUNKS, drain_z, 0)
 
 
 def window(cap, group, base, number, residuals, codes, ids, rotation, codebook):
@@ -373,7 +385,7 @@
             pltpu.VMEM((PEERS, 1, lanes), jnp.int32),
             pltpu.VMEM((PEERS, 1, lanes), jnp.int32),
             pltpu.VMEM((ZS, LISTS, PEERS * cap), BF),
-            pltpu.VMEM((3, 4, 2, LISTS, WIDTH), F32),
+            pltpu.VMEM((5, 4, 2, LISTS, WIDTH), F32),
             pltpu.VMEM((CHUNKS, 2, 2, 4, HALF, WIDTH), BF),
             pltpu.VMEM((CHUNKS, 2, 2, 4, HALF, WIDTH), BF),
             pltpu.VMEM((ZS, 1, LISTS), F32),

time: 82.3 us -> 78.2 us (0.950)
  Pallas kernels: 77.3 us -> 72.9 us
    pallas_call x1, Pallas kernels: 77.3 us -> 72.9 us  [window(): pl.pallas_call(functools.partial(window_kernel, cap, group, base), out_sh...]
where the time goes in v4:
time: 78.2 us; the launch traced here: 77.1 us
  Pallas kernels  72.9 us (93%)
  other arithmetic  1.58 us (2%)
  between operations  1.35 us (2%)
  local copies, waits for them, and re-layouts  1.05 us (1%)
    pallas_call x1, Pallas kernels, window(): pl.pallas_call(functools.partial(window_kernel, cap, group, base), out_sh...  72.9 us

profile of v4, /device:TPU:2, one launch (start us, length us, event | category | flops | bytes accessed | tf_op | source)
XLA Modules:
  0.0 77.1 jit_solution(16631489388681442422)
XLA Ops:
  0.6 0.0 copy-start
  0.6 72.9 %shard_map.85 = (f32[256,768]{1,0:T(8,128)S(1)}, s32[1,256]{1,0:T(1,128)S(1)}, s32[1,128]{1,0:T(1,128)}) custom-call(bf16[1024,768]{1,0:T(8,128)(2,1)} %res_hbm.1, s32[64,1024]{1,0:T(8,128)} %bitcast.5, s32[1,1024]{1,0:T(1,128)} %bitcast.7, bf16[768,768]{1,0:T(8,128)(2,1)} %rot_hbm.1, bf16[256,768]{1,0:T(8,128)(2,1)} %book_hbm.1), custom_call_target="tpu_custom_call" | custom-call | tf_op jit(solution)/shard_map/pallas_call | solution.py:362
  74.3 0.0 copy-done
  74.3 0.0 copy-start.2
  74.3 0.2 conditional.1
  74.5 0.5 copy-done.2
  74.9 0.6 fusion
  75.5 1.0 %broadcast_divide_fusion = f32[256,768]{1,0:T(8,128)} fusion(f32[256,768]{1,0:T(8,128)S(1)} %get-tuple-element.64, f32[256]{0:T(256)S(1)} %get-tuple-element.67), kind=kLoop, calls=%fused_computation | loop fusion | flops 196608 | bytes 1573888 | tf_op jit(solution)/shard_map/div | solution.py:417
  76.5 0.6 copy.14
Async XLA Ops:
  0.6 73.6 %copy-start = (s32[1024]{0:T(1024)S(1)}, s32[1024]{0:T(1024)}, u32[]{:S(2)}) copy-start(s32[1024]{0:T(1024)} %param.10) | copy-start | bytes 12292
  74.3 0.7 copy-start.2
